TPU v7x, 32 devices: a whole 2x2x4 slice. The times are simulated.
32 devices in a mesh: groups: 2 (over y), samples: 8 (over z, x), section: 1, mp: 2 (over core).
Axes of the slice: x: 2, y: 2, z: 4, core: 2. Of those that a mesh axis runs over, the one named last changes fastest.
Arguments:
- stored_inputs: bfloat16 [1, 16, 128, 2048], P('section', ('groups', 'samples'), None, 'mp'), parts along dimension 1
- top_cotangent: bfloat16 [16, 128, 2048], P(('groups', 'samples'), None, 'mp'), parts along dimension 0, may hold values from -0.375 to 0.375
- layer_weights: bfloat16 [1, 2048, 2048], P('section', 'samples', 'mp'), may hold values from -0.125 to 0.125
- block_layout: int32 [1, 2, 2], P('section'), may hold values 0 or 1
- region_mask: int32 [128], replicated, may hold values from 0 to 1, as said below
- partner_samples: int32 [16], P('groups'), parts along dimension 0, may hold values from 0 to 7, as said below
- spins: int32 [16, 128], P(('groups', 'samples')), parts along dimension 0, may hold values from 0 to 1
Outputs:
- weight_grad: float32 [2, 2048, 2048], P(('groups', 'section'), 'samples', 'mp'), parts along dimension 0
- layer_cotangents: bfloat16 [1, 16, 128, 2048], P('section', ('groups', 'samples'), None, 'mp'), parts along dimension 1
- embed_grad: float32 [4, 2048], P('groups', 'mp'), parts along dimension 0
There are 2 independent parts, one for each index of `groups`. A program takes and returns all parts, laid end to end along the dimension named above; an argument that names none is the same for every part. Nothing has to cross between parts.
Inputs may be any that keep to these rules, and one draw needn't show every extreme that they name: `region_mask`: exactly 64 of the 128 entries are 1, the others 0. The samples pair up: partner_samples[partner_samples[r]] = r and partner_samples[r] != r for every sample r. `block_layout`: a query block always sees its own block, whatever the diagonal entry holds.
All inputs are finite; a program needn't handle non-finite values.
Results may differ from a plain program's by a relative error of at most 0.03.
Values may be sent and summed in bfloat16 or wider, within the bound.
A program may use at most 64 MiB of HBM per device.

v0:
```python
import jax
import jax.numpy as jnp
from jax import lax
from jax.sharding import PartitionSpec as P

HEAD = 128
BLOCK = 64
SPINS = 2


def for_sending(value):

    def short(part):
        return part.astype(jnp.bfloat16) if part.dtype == jnp.float32 else part

    return jax.tree.map(short, value)


def passed_along(block, axis, distance):
    devices = range(lax.axis_size(axis))
    route = [(i - distance, i) for i in devices if i - distance in devices]
    return lax.ppermute(block, axis, route)


def softmax_parts(inputs_h, allowed, attention_scale):
    scores = (
        jnp.einsum("qhd,khd->hqk", inputs_h, inputs_h, preferred_element_type=jnp.float32)
        * attention_scale
    )
    scores = jnp.where(allowed[None], scores, -jnp.inf)
    top_score = jnp.max(scores, axis=-1, keepdims=True)
    expo_terms = jnp.exp(scores - top_score)
    probs = expo_terms / jnp.sum(expo_terms, axis=-1, keepdims=True)
    return (probs, probs.astype(jnp.bfloat16))


def local(
    stored_inputs, top_cotangent, layer_weights, block_layout, region_mask, partner_samples, spins
):
    section_index = lax.axis_index("section")
    section_count = lax.axis_size("section")
    micro_count = stored_inputs.shape[1]
    seq_len = stored_inputs.shape[2]
    half_width = stored_inputs.shape[3]
    head_count = half_width // HEAD
    attention_scale = 4.0 / HEAD
    weights = lax.all_gather(layer_weights[0], "samples", axis=0, tiled=True)
    pos_block = jnp.arange(seq_len) // BLOCK
    block_onehot = (pos_block[:, None] == jnp.arange(block_layout.shape[1])[None, :]).astype(
        jnp.float32
    )
    linked = jnp.dot(jnp.dot(block_onehot, block_layout[0].astype(jnp.float32)), block_onehot.T)
    allowed = (linked > 0.5) | (pos_block[:, None] == pos_block[None, :])
    every_layer_input = stored_inputs[0]
    inputs_h = every_layer_input[0].reshape(seq_len, head_count, HEAD)
    probs, probs_low = softmax_parts(inputs_h, allowed, attention_scale)
    attended = jnp.einsum(
        "hqk,khd->qhd", probs_low, inputs_h, preferred_element_type=jnp.float32
    ).astype(jnp.bfloat16)
    probs_list = [probs]
    low_list = [probs_low]
    attend_list = [attended.reshape(seq_len, half_width)]
    probs_all = jnp.stack(probs_list)
    low_all = jnp.stack(low_list)
    attend_store = jnp.stack(attend_list)

    def layer_back(grad_full, grad_own, inputs, probs, probs_low):
        grad_attn = jnp.dot(grad_full, weights, preferred_element_type=jnp.float32).astype(
            jnp.bfloat16
        )
        inputs_h = inputs.reshape(seq_len, head_count, HEAD)
        grad_h = grad_attn.reshape(seq_len, head_count, HEAD)
        grad_probs = jnp.einsum(
            "qhd,khd->hqk", grad_h, inputs_h, preferred_element_type=jnp.float32
        )
        grad_scores = (
            probs * (grad_probs - jnp.sum(grad_probs * probs, axis=-1, keepdims=True))
        ).astype(jnp.bfloat16)
        through = jnp.einsum("hqk,qhd->khd", probs_low, grad_h, preferred_element_type=jnp.float32)
        through = through + attention_scale * (
            jnp.einsum("hqk,khd->qhd", grad_scores, inputs_h, preferred_element_type=jnp.float32)
            + jnp.einsum("hqk,qhd->khd", grad_scores, inputs_h, preferred_element_type=jnp.float32)
        )
        grad_in = grad_own.astype(jnp.float32) + through.reshape(seq_len, half_width)
        return grad_in.astype(jnp.bfloat16)

    def resting(grad_full, grad_own, inputs, probs, probs_low):
        return jnp.zeros((seq_len, half_width), jnp.bfloat16)

    carried_state = jnp.zeros((seq_len, half_width), jnp.bfloat16)
    out_list = []
    grad_list = []
    total_steps = micro_count + section_count - 1
    for step_number in range(total_steps):
        micro_index = step_number - (section_count - 1 - section_index)
        active = (micro_index >= 0) & (micro_index < micro_count)
        slot_index = jnp.clip(micro_index, 0, micro_count - 1)
        from_top = lax.dynamic_index_in_dim(top_cotangent, slot_index, 0, keepdims=False)
        incoming = jnp.where(section_index == section_count - 1, from_top, carried_state)
        grad_full = lax.all_gather(incoming, "mp", axis=1, tiled=True)
        inputs_now = lax.dynamic_index_in_dim(every_layer_input, slot_index, 0, keepdims=False)
        probs_now = lax.dynamic_index_in_dim(probs_all, slot_index, 0, keepdims=False)
        low_now = lax.dynamic_index_in_dim(low_all, slot_index, 0, keepdims=False)
        grad_in = lax.cond(
            active, layer_back, resting, grad_full, incoming, inputs_now, probs_now, low_now
        )
        out_list.append(grad_in)
        grad_list.append(grad_full)
        if step_number < total_steps - 1:
            carried_state = jax.tree.map(
                lambda part, own: part.astype(own.dtype),
                passed_along(for_sending(grad_in), "section", -1),
                grad_in,
            )
    offset = section_count - 1 - section_index
    out_store = lax.dynamic_slice_in_dim(jnp.stack(out_list), offset, micro_count, 0)
    grad_store = lax.dynamic_slice_in_dim(jnp.stack(grad_list), offset, micro_count, 0)
    summed_weight = lax.psum_scatter(
        jnp.einsum(
            "mtf,mta->fa", grad_store, attend_store, preferred_element_type=jnp.float32
        ).astype(jnp.bfloat16),
        "samples",
        scatter_dimension=0,
        tiled=True,
    ).astype(jnp.float32)
    region_count = seq_len // 2
    rank_in_region = jnp.cumsum(region_mask) - 1
    select = (
        (rank_in_region[None, :] == jnp.arange(region_count)[:, None]) & (region_mask[None, :] > 0)
    ).astype(jnp.bfloat16)
    tiles = jnp.einsum("at,mtd->mad", select, out_store, preferred_element_type=jnp.float32).astype(
        jnp.bfloat16
    )
    shard_index = lax.axis_index("samples")
    my_partners = lax.dynamic_slice_in_dim(
        partner_samples, shard_index * micro_count, micro_count, 0
    )
    shard_count = lax.axis_size("samples")
    dest_shard = my_partners // micro_count
    dest_slot = my_partners % micro_count
    route = (
        (dest_shard[:, None, None] == jnp.arange(shard_count)[None, :, None])
        & (dest_slot[:, None, None] == jnp.arange(micro_count)[None, None, :])
    ).astype(jnp.bfloat16)
    outgoing = jnp.einsum("mku,mad->kuad", route, tiles, preferred_element_type=jnp.float32).astype(
        jnp.bfloat16
    )
    arrived = lax.all_to_all(outgoing, "samples", split_axis=0, concat_axis=0, tiled=True)
    ones_row = jnp.ones((shard_count,), jnp.bfloat16)
    received = jnp.einsum(
        "k,kuad->uad", ones_row, arrived, preferred_element_type=jnp.float32
    ).astype(jnp.bfloat16)
    placed = jnp.einsum("at,mad->mtd", select, received, preferred_element_type=jnp.float32)
    kept = jnp.where(region_mask[None, :, None] > 0, jnp.zeros_like(out_store), out_store)
    site_cot = (kept.astype(jnp.float32) + placed).astype(jnp.bfloat16)
    cotangents = jnp.where(section_index == 0, site_cot, out_store)
    onehot = (spins[:, :, None] == jnp.arange(SPINS)[None, None, :]).astype(jnp.bfloat16)
    embed_term = jnp.einsum("mtv,mtd->vd", onehot, site_cot, preferred_element_type=jnp.float32)
    embed_term = jnp.where(section_index == 0, embed_term, jnp.zeros_like(embed_term))
    embed_grad = lax.psum(embed_term, ("samples", "section"))
    return (summed_weight[None], cotangents[None], embed_grad)


def solution(mesh):
    in_specs = (
        P("section", ("groups", "samples"), None, "mp"),
        P(("groups", "samples"), None, "mp"),
        P("section", "samples", "mp"),
        P("section", None, None),
        P(),
        P("groups"),
        P(("groups", "samples"), None),
    )
    out_specs = (
        P(("groups", "section"), "samples", "mp"),
        P("section", ("groups", "samples"), None, "mp"),
        P("groups", "mp"),
    )
    return jax.shard_map(local, mesh=mesh, in_specs=in_specs, out_specs=out_specs, check_vma=False)
```

profile of v0, /device:TPU:0, one launch (start us, length us, event | category | flops | bytes accessed | tf_op | source)
XLA Modules:
  0.0 230.9 jit_solution(3617918182335922141)
XLA Ops:
  7.2 0.0 all-gather.4.cloned.1.call-start
  7.2 0.7 all-gather.4.cloned.1.call-update
  7.9 0.0 reduce-scatter.2.cloned.1.call-start
  8.0 1.1 fusion.20
  9.1 0.1 copy.44
  9.2 1.0 copy.68
  10.2 0.2 copy.48
  10.4 2.5 %all-gather = bf16[1,128,2048]{2,1,0:T(8,128)(2,1)S(1)} all-gather(bf16[1,128,1024]{2,1,0:T(8,128)(2,1)} %param.8), channel_id=2, replica_groups=mesh['groups'=2,'samples'=8,'section'=1,'mp'=2] {'mp'}, dimensions={2}, use_global_device_ids=true | all-gather | bytes 786432 | tf_op jit(solution)/shard_map/all_gather | solution.py:100
  13.0 0.4 fusion.78
  13.3 0.5 convolution_convert_fusion
  13.9 0.0 copy-start
  13.9 3.2 %convert_bitcast_fusion = bf16[2048,1024]{0,1:T(8,128)(2,1)} fusion(bf16[128,1024]{0,1:T(8,128)(2,1)S(1)} %bitcast.106, bf16[1,128,2048]{2,1,0:T(8,128)(2,1)S(1)} %all-gather), kind=kOutput, calls=%fused_computation.3 | convolution fusion | flops 538968064 | bytes 4980736 | tf_op jit(solution)/shard_map/mtf,mta->fa/dot_general | solution.py:119
  17.0 0.0 copy-start.1
  17.0 0.0 copy-start.3
  17.1 0.0 reduce-scatter.2.cloned.1.call-update
  17.1 0.0 copy-done
  17.1 0.2 copy.49
  17.3 0.4 copy-done.1
  17.7 0.1 copy.58
  17.8 0.2 reduce-window.8
  18.0 0.0 copy-done.3
  18.0 0.6 dynamic_slice.12
  18.6 0.6 fusion.61
  19.2 0.1 add_reduce_fusion
  19.3 66.3 %all-gather.4.cloned.1.call-done = bf16[1,2048,1024]{2,1,0:T(8,128)(2,1)} async-done(((bf16[1,256,1024]{2,1,0:T(8,128)(2,1)}), bf16[1,2048,1024]{2,1,0:T(8,128)(2,1)}) %all-gather.4.cloned.1.call-update) | async-done | bytes 4194320 | tf_op jit(solution)/shard_map/all_gather | solution.py:47
  85.6 2.9 %fusion.14 = bf16[16,8,8,128]{3,2,1,0:T(8,128)(2,1)S(1)} fusion(bf16[1,2048,1024]{2,1,0:T(8,128)(2,1)} %all-gather.4.cloned.1.call-done, bf16[1,128,2048]{2,1,0:T(8,128)(2,1)S(1)} %all-gather), kind=kOutput, calls=%fused_computation.19 | convolution fusion | flops 537001984 | bytes 4980736 | tf_op jit(solution)/shard_map/cond/branch_1_fun/dot_general | solution.py:68
  88.6 0.3 multiply_reduce_fusion
  88.9 0.1 multiply_convert_fusion.1
  89.0 0.3 fusion.81
  89.3 0.2 fusion.7
  89.5 0.5 fusion.5
  90.0 0.1 fusion.28
  90.1 0.2 fusion.19
  90.3 1.2 fusion.23
  91.5 0.0 copy-start.2
  91.5 3.7 %all-to-all-start = ((bf16[8,1,64,1024]{3,2,1,0:T(8,128)(2,1)}), bf16[8,1,64,1024]{3,2,1,0:T(8,128)(2,1)S(1)}, u32[]{:S(2)}, u32[]{:S(2)}) async-start(bf16[8,1,64,1024]{3,2,1,0:T(8,128)(2,1)} %fusion.23), calls=%async_computation.1 | async-start | bytes 2097152 | tf_op jit(solution)/shard_map/all_to_all | solution.py:148
  95.2 0.1 fusion.31
  95.3 103.4 %reduce-scatter.2.cloned.1.call-done = bf16[256,1024]{0,1:T(8,128)(2,1)} async-done(((bf16[2048,1024]{0,1:T(8,128)(2,1)}), bf16[256,1024]{0,1:T(8,128)(2,1)}) %reduce-scatter.2.cloned.1.call-update) | async-done | bytes 524304 | tf_op jit(solution)/shard_map/reduce_scatter | solution.py:118
  198.7 1.1 bitcast_convert_fusion
  199.8 1.3 copy.59
  201.1 0.0 all-to-all-done
  201.1 0.8 fusion.24
  201.9 0.3 fusion.10
  202.1 0.0 copy-done.2
  202.2 0.2 fusion.35
  202.3 20.9 %psum.7 = f32[2,1024]{1,0:T(2,128)} all-reduce(f32[2,1024]{1,0:T(2,128)S(1)} %fusion.35), channel_id=1, replica_groups=mesh['groups'=2,'samples'=8,'section'=1,'mp'=2] {'samples','section'}, use_global_device_ids=true, to_apply=%region_5.6 | all-reduce | flops 2048 | bytes 16384 | tf_op jit(solution)/shard_map/psum | solution.py:160
  223.2 0.8 copy.60
  (2 shorter events, 0.0 us)
Async XLA Ops:
  7.2 78.5 %all-gather.4.cloned.1.call-start = ((), (), s32[]{:S(2)}) async-start(), calls=%async_computation.3 | async-start | bytes 4718592 | tf_op jit(solution)/shard_map/all_gather | solution.py:47
  7.9 190.8 %reduce-scatter.2.cloned.1.call-start = ((), (), s32[]{:S(2)}) async-start(), calls=%async_computation.2 | async-start | bytes 4718592 | tf_op jit(solution)/shard_map/reduce_scatter | solution.py:118
  13.9 3.2 %copy-start = (bf16[1,128,1024]{2,1,0:T(8,128)(2,1)S(1)}, bf16[1,128,1024]{2,1,0:T(8,128)(2,1)}, u32[]{:S(2)}) copy-start(bf16[1,128,1024]{2,1,0:T(8,128)(2,1)} %param.8) | copy-start | bytes 786436
  17.0 0.7 copy-start.1
  17.0 0.9 copy-start.3
  91.5 110.6 %copy-start.2 = (s32[1,128]{1,0:T(1,128)S(1)}, s32[1,128]{1,0:T(1,128)}, u32[]{:S(2)}) copy-start(s32[1,128]{1,0:T(1,128)} %param.13) | copy-start | bytes 1540
  91.5 109.6 %all-to-all-start = ((bf16[8,1,64,1024]{3,2,1,0:T(8,128)(2,1)}), bf16[8,1,64,1024]{3,2,1,0:T(8,128)(2,1)S(1)}, u32[]{:S(2)}, u32[]{:S(2)}) async-start(bf16[8,1,64,1024]{3,2,1,0:T(8,128)(2,1)} %fusion.23), calls=%async_computation.1 | async-start | bytes 2097152 | tf_op jit(solution)/shard_map/all_to_all | solution.py:148
Sparse Core Ops, SparseCore 0:
  10.1 75.4 all-gather.3
  89.3 109.3 reduce-scatter.1
where the time goes:
time: 231 us
  waiting for transfers between devices  170 us (74%)
  blocking collectives  23.4 us (10%)
  between operations  14.2 us (6%)
  matrix products  10.9 us (5%)
  local copies, waits for them, and re-layouts  4.81 us (2%)
  starting transfers between devices  3.76 us (2%)
  other arithmetic  3.48 us (2%)
    reduce_scatter x1, waiting for transfers between devices, local(): lax.psum_scatter(jnp.einsum('mtf,mta->fa', grad_store, attend_store, pref...  103 us
    all_gather x1, waiting for transfers between devices, local(): weights = lax.all_gather(layer_weights[0], 'samples', axis=0, tiled=True)  66.3 us
    psum x1, blocking collectives, local(): embed_grad = lax.psum(embed_term, ('samples', 'section'))  20.9 us
  transfers between devices with their start and end apart: 3, of which 2 were waited for; matrix products, arithmetic and copies ran while one was open for 7% of the time, Pallas kernels for 0%

commit v1 on v0

--- a/solution.py
+++ b/solution.py
@@ -157,7 +157,8 @@
     onehot = (spins[:, :, None] == jnp.arange(SPINS)[None, None, :]).astype(jnp.bfloat16)
     embed_term = jnp.einsum("mtv,mtd->vd", onehot, site_cot, preferred_element_type=jnp.float32)
     embed_term = jnp.where(section_index == 0, embed_term, jnp.zeros_like(embed_term))
-    embed_grad = lax.psum(embed_term, ("samples", "section"))
+    partial = lax.psum(embed_term, "section")
+    embed_grad = lax.psum(partial, "samples")
     return (summed_weight[None], cotangents[None], embed_grad)
 
 

time: 231 us -> 231 us (level)
  no operation moved by 1% of the time
where the time goes in v1:
time: 231 us
  waiting for transfers between devices  170 us (74%)
  blocking collectives  23.4 us (10%)
  between operations  14.2 us (6%)
  matrix products  10.9 us (5%)
  local copies, waits for them, and re-layouts  4.81 us (2%)
  starting transfers between devices  3.76 us (2%)
  other arithmetic  3.48 us (2%)
    reduce_scatter x1, waiting for transfers between devices, local(): lax.psum_scatter(jnp.einsum('mtf,mta->fa', grad_store, attend_store, pref...  103 us
    all_gather x1, waiting for transfers between devices, local(): weights = lax.all_gather(layer_weights[0], 'samples', axis=0, tiled=True)  66.3 us
    psum x1, blocking collectives, local(): embed_grad = lax.psum(partial, 'samples')  20.9 us
  transfers between devices with their start and end apart: 3, of which 2 were waited for; matrix products, arithmetic and copies ran while one was open for 7% of the time, Pallas kernels for 0%

profile of v1, /device:TPU:0, one launch (start us, length us, event | category | flops | bytes accessed | tf_op | source)
XLA Modules:
  0.0 230.9 jit_solution(3617918182335922141)
XLA Ops:
  7.2 0.0 all-gather.4.cloned.1.call-start
  7.2 0.7 all-gather.4.cloned.1.call-update
  7.9 0.0 reduce-scatter.2.cloned.1.call-start
  8.0 1.1 fusion.20
  9.1 0.1 copy.44
  9.2 1.0 copy.68
  10.2 0.2 copy.48
  10.4 2.5 %all-gather = bf16[1,128,2048]{2,1,0:T(8,128)(2,1)S(1)} all-gather(bf16[1,128,1024]{2,1,0:T(8,128)(2,1)} %param.8), channel_id=2, replica_groups=mesh['groups'=2,'samples'=8,'section'=1,'mp'=2] {'mp'}, dimensions={2}, use_global_device_ids=true | all-gather | bytes 786432 | tf_op jit(solution)/shard_map/all_gather | solution.py:100
  13.0 0.4 fusion.78
  13.3 0.5 convolution_convert_fusion
  13.9 0.0 copy-start
  13.9 3.2 %convert_bitcast_fusion = bf16[2048,1024]{0,1:T(8,128)(2,1)} fusion(bf16[128,1024]{0,1:T(8,128)(2,1)S(1)} %bitcast.106, bf16[1,128,2048]{2,1,0:T(8,128)(2,1)S(1)} %all-gather), kind=kOutput, calls=%fused_computation.3 | convolution fusion | flops 538968064 | bytes 4980736 | tf_op jit(solution)/shard_map/mtf,mta->fa/dot_general | solution.py:119
  17.0 0.0 copy-start.1
  17.0 0.0 copy-start.3
  17.1 0.0 reduce-scatter.2.cloned.1.call-update
  17.1 0.0 copy-done
  17.1 0.2 copy.49
  17.3 0.4 copy-done.1
  17.7 0.1 copy.58
  17.8 0.2 reduce-window.8
  18.0 0.0 copy-done.3
  18.0 0.6 dynamic_slice.12
  18.6 0.6 fusion.61
  19.2 0.1 add_reduce_fusion
  19.3 66.3 %all-gather.4.cloned.1.call-done = bf16[1,2048,1024]{2,1,0:T(8,128)(2,1)} async-done(((bf16[1,256,1024]{2,1,0:T(8,128)(2,1)}), bf16[1,2048,1024]{2,1,0:T(8,128)(2,1)}) %all-gather.4.cloned.1.call-update) | async-done | bytes 4194320 | tf_op jit(solution)/shard_map/all_gather | solution.py:47
  85.6 2.9 %fusion.14 = bf16[16,8,8,128]{3,2,1,0:T(8,128)(2,1)S(1)} fusion(bf16[1,2048,1024]{2,1,0:T(8,128)(2,1)} %all-gather.4.cloned.1.call-done, bf16[1,128,2048]{2,1,0:T(8,128)(2,1)S(1)} %all-gather), kind=kOutput, calls=%fused_computation.19 | convolution fusion | flops 537001984 | bytes 4980736 | tf_op jit(solution)/shard_map/cond/branch_1_fun/dot_general | solution.py:68
  88.6 0.3 multiply_reduce_fusion
  88.9 0.1 multiply_convert_fusion.1
  89.0 0.3 fusion.81
  89.3 0.2 fusion.7
  89.5 0.5 fusion.5
  90.0 0.1 fusion.28
  90.1 0.2 fusion.19
  90.3 1.2 fusion.23
  91.5 0.0 copy-start.2
  91.5 3.7 %all-to-all-start = ((bf16[8,1,64,1024]{3,2,1,0:T(8,128)(2,1)}), bf16[8,1,64,1024]{3,2,1,0:T(8,128)(2,1)S(1)}, u32[]{:S(2)}, u32[]{:S(2)}) async-start(bf16[8,1,64,1024]{3,2,1,0:T(8,128)(2,1)} %fusion.23), calls=%async_computation.1 | async-start | bytes 2097152 | tf_op jit(solution)/shard_map/all_to_all | solution.py:148
  95.2 0.1 fusion.31
  95.3 103.4 %reduce-scatter.2.cloned.1.call-done = bf16[256,1024]{0,1:T(8,128)(2,1)} async-done(((bf16[2048,1024]{0,1:T(8,128)(2,1)}), bf16[256,1024]{0,1:T(8,128)(2,1)}) %reduce-scatter.2.cloned.1.call-update) | async-done | bytes 524304 | tf_op jit(solution)/shard_map/reduce_scatter | solution.py:118
  198.7 1.1 bitcast_convert_fusion
  199.8 1.3 copy.59
  201.1 0.0 all-to-all-done
  201.1 0.8 fusion.24
  201.9 0.3 fusion.10
  202.1 0.0 copy-done.2
  202.2 0.2 fusion.35
  202.3 20.9 %psum.6 = f32[2,1024]{1,0:T(2,128)} all-reduce(f32[2,1024]{1,0:T(2,128)S(1)} %fusion.35), channel_id=1, replica_groups=mesh['groups'=2,'samples'=8,'section'=1,'mp'=2] {'samples'}, use_global_device_ids=true, to_apply=%region_5.6 | all-reduce | flops 2048 | bytes 16384 | tf_op jit(solution)/shard_map/psum | solution.py:161
  223.2 0.8 copy.60
  (2 shorter events, 0.0 us)
Async XLA Ops:
  7.2 78.5 %all-gather.4.cloned.1.call-start = ((), (), s32[]{:S(2)}) async-start(), calls=%async_computation.3 | async-start | bytes 4718592 | tf_op jit(solution)/shard_map/all_gather | solution.py:47
  7.9 190.8 %reduce-scatter.2.cloned.1.call-start = ((), (), s32[]{:S(2)}) async-start(), calls=%async_computation.2 | async-start | bytes 4718592 | tf_op jit(solution)/shard_map/reduce_scatter | solution.py:118
  13.9 3.2 %copy-start = (bf16[1,128,1024]{2,1,0:T(8,128)(2,1)S(1)}, bf16[1,128,1024]{2,1,0:T(8,128)(2,1)}, u32[]{:S(2)}) copy-start(bf16[1,128,1024]{2,1,0:T(8,128)(2,1)} %param.8) | copy-start | bytes 786436
  17.0 0.7 copy-start.1
  17.0 0.9 copy-start.3
  91.5 110.6 %copy-start.2 = (s32[1,128]{1,0:T(1,128)S(1)}, s32[1,128]{1,0:T(1,128)}, u32[]{:S(2)}) copy-start(s32[1,128]{1,0:T(1,128)} %param.13) | copy-start | bytes 1540
  91.5 109.6 %all-to-all-start = ((bf16[8,1,64,1024]{3,2,1,0:T(8,128)(2,1)}), bf16[8,1,64,1024]{3,2,1,0:T(8,128)(2,1)S(1)}, u32[]{:S(2)}, u32[]{:S(2)}) async-start(bf16[8,1,64,1024]{3,2,1,0:T(8,128)(2,1)} %fusion.23), calls=%async_computation.1 | async-start | bytes 2097152 | tf_op jit(solution)/shard_map/all_to_all | solution.py:148
Sparse Core Ops, SparseCore 0:
  10.1 75.4 all-gather.3
  89.3 109.3 reduce-scatter.1
